TPU v7x, 512 devices: a whole 4x4x16 slice. The times are simulated.
512 devices in a mesh: dp: 128 (over z, x, core), layer: 4 (over y).
Axes of the slice: x: 4, y: 4, z: 16, core: 2. Of those that a mesh axis runs over, the one named last changes fastest.
Arguments:
- micro_grads: bfloat16 [4, 128, 256, 2048], P('layer', 'dp')
- master: float32 [4, 384, 2, 2048], P('layer', 'dp'), may hold values from -6 to 6
- moment_one: float32 [4, 384, 2, 2048], P('layer', 'dp'), may hold values from -4 to 4
- moment_two: float32 [4, 384, 2, 2048], P('layer', 'dp'), may hold values from 0.01 to 1
- owner: int32 [4, 128], P('layer'), may hold values from 0 to 127, as said below
- slot: int32 [4, 128], P('layer'), may hold values from 0 to 2, as said below
Outputs:
- new_master: float32 [4, 384, 2, 2048], P('layer', 'dp')
- new_moment_one: float32 [4, 384, 2, 2048], P('layer', 'dp')
- new_moment_two: float32 [4, 384, 2, 2048], P('layer', 'dp')
- weights: bfloat16 [4, 256, 2048], P('layer')
- grad_rms: float32 [], replicated
Inputs may be any that keep to these rules, and one draw needn't show every extreme that they name: In every layer no owner holds more than 3 blocks, and some owner holds exactly 3. The pairs (owner, slot) of one layer are all different.
All inputs are finite; a program needn't handle non-finite values.
Results may differ from a plain program's by a relative error of at most 0.0004.
Values may be sent and summed in bfloat16 or wider, within the bound.
No kernel may reach another device: no remote copies, remote signals or barrier semaphores. Data moves between devices by JAX's collectives and lax.ppermute only.
A program may use at most 64 MiB of HBM per device.

v0:
```python
import jax
import jax.numpy as jnp
from jax import lax
from jax.sharding import PartitionSpec as P

beta_one = 0.9
beta_two = 0.95
learn_rate = 0.0003
decay_rate = 0.1
adam_eps = 1e-08
step_number = 100.0


def adamw(param, first, second, grad):
    first_new = beta_one * first + (1.0 - beta_one) * grad
    second_new = beta_two * second + (1.0 - beta_two) * grad * grad
    corr_one = 1.0 - beta_one**step_number
    corr_two = 1.0 - beta_two**step_number
    update = (
        first_new / corr_one / (jnp.sqrt(second_new / corr_two) + adam_eps) + decay_rate * param
    )
    return (param - learn_rate * update, first_new, second_new)


def shards(micro_grads, master, moment_one, moment_two, owner, slot):
    my_index = lax.axis_index("dp")
    row_count = micro_grads.shape[2]
    feature_count = micro_grads.shape[3]
    capacity = master.shape[1]
    slab_rows = master.shape[2]
    block_count = owner.shape[1]
    summed = micro_grads[0, 0].astype(jnp.float32)
    flat_grad = summed.reshape(-1, 128)
    grad_share = lax.psum_scatter(flat_grad, "dp", scatter_dimension=0, tiled=True)
    reduced = lax.all_gather(grad_share, "dp", axis=0, tiled=True).reshape(row_count, feature_count)
    squares = lax.psum(jnp.sum(grad_share * grad_share), ("dp", "layer"))
    element_total = lax.axis_size("layer") * row_count * feature_count
    grad_rms = jnp.sqrt(squares / element_total + 1e-06)
    clip_factor = jnp.minimum(1.0, 1.0 / grad_rms)
    owners = owner[0]
    slots_of = slot[0]
    slot_ids = jnp.arange(capacity, dtype=jnp.int32)
    matches = (owners[None, :] == my_index) & (slots_of[None, :] == slot_ids[:, None])
    filled = jnp.any(matches, axis=1)
    block_of_slot = jnp.sum(
        jnp.where(matches, jnp.arange(block_count, dtype=jnp.int32)[None, :], 0), axis=1
    )
    blocks_grad = reduced.reshape(block_count, slab_rows, feature_count)
    grad_slots = jnp.take(blocks_grad, block_of_slot, axis=0) * clip_factor
    param, first, second = adamw(master[0], moment_one[0], moment_two[0], grad_slots)
    keep = filled[:, None, None]
    new_master = jnp.where(keep, param, master[0])
    new_first = jnp.where(keep, first, moment_one[0])
    new_second = jnp.where(keep, second, moment_two[0])
    slot_weights = param.astype(jnp.bfloat16)
    mine = owners == my_index
    block_weights = jnp.take(slot_weights, slots_of, axis=0)
    placed = jnp.where(mine[:, None, None], block_weights.astype(jnp.float32), 0.0).reshape(-1, 128)
    weight_share = lax.psum_scatter(placed, "dp", scatter_dimension=0, tiled=True).astype(
        jnp.bfloat16
    )
    weights = lax.all_gather(weight_share, "dp", axis=0, tiled=True).reshape(
        row_count, feature_count
    )
    return (new_master[None], new_first[None], new_second[None], weights[None], grad_rms)


def solution(mesh):
    in_specs = (
        P("layer", "dp", None, None),
        P("layer", "dp", None, None),
        P("layer", "dp", None, None),
        P("layer", "dp", None, None),
        P("layer", None),
        P("layer", None),
    )
    out_specs = (
        P("layer", "dp", None, None),
        P("layer", "dp", None, None),
        P("layer", "dp", None, None),
        P("layer", None, None),
        P(),
    )
    return jax.shard_map(shards, mesh=mesh, in_specs=in_specs, out_specs=out_specs, check_vma=False)
```

profile of v0, /device:TPU:1, one launch (start us, length us, event | category | flops | bytes accessed | tf_op | source)
XLA Modules:
  0.0 830.3 jit_solution(17510532060689569105)
XLA Ops:
  7.2 0.0 reduce-scatter.3.cloned.1.call-start
  7.2 2.6 reshape.111
  9.9 0.0 all-gather.3.cloned.1.call-start
  9.9 258.4 %reduce-scatter.3.cloned.1.call-done = f32[32,128]{1,0:T(8,128)} async-done(((f32[4096,128]{1,0:T(8,128)}), f32[32,128]{1,0:T(8,128)}) %reduce-scatter.3.cloned.1.call-update) | async-done | bytes 16400 | tf_op jit(solution)/shard_map/reduce_scatter | solution.py:34
  268.3 0.0 reduce-scatter.5.cloned.1.call-start
  268.4 0.1 select_reduce_fusion
  268.6 1.3 multiply_reduce_fusion
  269.9 113.3 %psum.7 = f32[]{:T(128)} all-reduce(f32[]{:T(128)} %multiply_reduce_fusion), channel_id=1, replica_groups=mesh['dp'=128,'layer'=4] {'dp','layer'}, use_global_device_ids=true, to_apply=%region_4.5 | all-reduce | flops 1 | bytes 8 | tf_op jit(solution)/shard_map/psum | solution.py:36
  384.0 36.3 %all-gather.3.cloned.1.call-done = f32[4096,128]{1,0:T(8,128)} async-done(((f32[32,128]{1,0:T(8,128)}), f32[4096,128]{1,0:T(8,128)}) %all-gather.3.cloned.1.call-update) | async-done | bytes 2097168 | tf_op jit(solution)/shard_map/all_gather | solution.py:35
  420.3 2.3 reshape_reshape.3
  422.6 0.6 gather_fusion
  423.2 0.3 fusion.9
  423.5 2.7 gather_fusion.1
  426.2 2.0 convert_select_fusion
  428.2 2.7 select_n.93
  430.9 0.0 reduce-scatter.5.cloned.1.call-update
  430.9 0.0 all-gather.5.cloned.1.call-start
  431.0 246.3 %reduce-scatter.5.cloned.1.call-done = f32[32,128]{1,0:T(8,128)} async-done(((f32[4096,128]{1,0:T(8,128)}), f32[32,128]{1,0:T(8,128)}) %reduce-scatter.5.cloned.1.call-update) | async-done | bytes 16400 | tf_op jit(solution)/shard_map/reduce_scatter | solution.py:59
  677.2 1.3 convert_element_type.22
  678.6 0.0 all-gather.5.cloned.1.call-update
  678.6 0.1 fusion.11
  678.7 1.0 broadcast_select_fusion.1
  679.7 140.7 %all-gather.5.cloned.1.call-done = bf16[4096,128]{1,0:T(8,128)(2,1)} async-done(((bf16[32,128]{1,0:T(8,128)(2,1)}), bf16[4096,128]{1,0:T(8,128)(2,1)}) %all-gather.5.cloned.1.call-update) | async-done | bytes 1048592 | tf_op jit(solution)/shard_map/all_gather | solution.py:62
  820.3 2.3 broadcast_in_dim_reshape.3
  (19 shorter events, 0.1 us)
Async XLA Ops:
  7.2 261.2 %copy-start.4 = (s32[1,128]{1,0:T(1,128)S(1)}, s32[1,128]{1,0:T(1,128)}, u32[]{:S(2)}) copy-start(s32[1,128]{1,0:T(1,128)} %param.11) | copy-start | bytes 1540
  7.2 261.2 %copy-start.3 = (s32[1,128]{1,0:T(1,128)S(1)}, s32[1,128]{1,0:T(1,128)}, u32[]{:S(2)}) copy-start(s32[1,128]{1,0:T(1,128)} %param.10) | copy-start | bytes 1540
  7.2 261.1 %reduce-scatter.3.cloned.1.call-start = ((), (), s32[]{:S(2)}) async-start(), calls=%async_computation.2 | async-start | bytes 2113536 | tf_op jit(solution)/shard_map/reduce_scatter | solution.py:34
  9.9 410.4 %all-gather.3.cloned.1.call-start = ((), (), s32[]{:S(2)}) async-start(), calls=%async_computation.3 | async-start | bytes 2113536 | tf_op jit(solution)/shard_map/all_gather | solution.py:35
  268.3 408.9 %reduce-scatter.5.cloned.1.call-start = ((), (), s32[]{:S(2)}) async-start(), calls=%async_computation.4 | async-start | bytes 2113536 | tf_op jit(solution)/shard_map/reduce_scatter | solution.py:59
  383.9 39.3 %copy-start = (f32[1,3,2,2048]{3,2,1,0:T(2,128)S(1)}, f32[1,3,2,2048]{3,2,1,0:T(2,128)}, u32[]{:S(2)}) copy-start(f32[1,3,2,2048]{3,2,1,0:T(2,128)} %param.9) | copy-start | bytes 147460
  384.0 39.3 %copy-start.1 = (f32[1,3,2,2048]{3,2,1,0:T(2,128)S(1)}, f32[1,3,2,2048]{3,2,1,0:T(2,128)}, u32[]{:S(2)}) copy-start(f32[1,3,2,2048]{3,2,1,0:T(2,128)} %param.7) | copy-start | bytes 147460
  384.0 39.3 %copy-start.2 = (f32[1,3,2,2048]{3,2,1,0:T(2,128)S(1)}, f32[1,3,2,2048]{3,2,1,0:T(2,128)}, u32[]{:S(2)}) copy-start(f32[1,3,2,2048]{3,2,1,0:T(2,128)} %param.8) | copy-start | bytes 147460
  430.9 389.4 %all-gather.5.cloned.1.call-start = ((), (), s32[]{:S(2)}) async-start(), calls=%async_computation.5 | async-start | bytes 1056768 | tf_op jit(solution)/shard_map/all_gather | solution.py:62
Sparse Core Ops, SparseCore 0:
  12.6 255.6 reduce-scatter.2
  271.4 148.7 all-gather.2
  431.1 246.1 reduce-scatter.4
  680.6 139.6 all-gather.4
where the time goes:
time: 831 us; the launch traced here: 830 us
  waiting for transfers between devices  682 us (82%)
  blocking collectives  113 us (14%)
  between operations  15.8 us (2%)
  local copies, waits for them, and re-layouts  13.3 us (2%)
    reduce_scatter x1, waiting for transfers between devices, shards(): lax.psum_scatter(flat_grad, 'dp', scatter_dimension=0, tiled=True)  258 us
    reduce_scatter x1, waiting for transfers between devices, shards(): lax.psum_scatter(placed, 'dp', scatter_dimension=0, tiled=True)  246 us
    all_gather x1, waiting for transfers between devices, shards(): lax.all_gather(weight_share, 'dp', axis=0, tiled=True)  141 us
    psum x1, blocking collectives, shards(): squares = lax.psum(jnp.sum(grad_share * grad_share), ('dp', 'layer'))  113 us
    all_gather x1, waiting for transfers between devices, shards(): lax.all_gather(grad_share, 'dp', axis=0, tiled=True)  36.3 us
  transfers between devices with their start and end apart: 4, of which 4 were waited for; matrix products, arithmetic and copies ran while one was open for 0% of the time, Pallas kernels for 0%

commit v1 on v0

--- a/solution.py
+++ b/solution.py
@@ -9,6 +9,12 @@
 decay_rate = 0.1
 adam_eps = 1e-08
 step_number = 100.0
+
+
+def push_the_cube(frame_in):
+    return jnp.concatenate(
+        lax.all_to_all(jnp.stack([frame_in] * lax.axis_size("dp")), "dp", 0, 0), axis=0
+    )
 
 
 def adamw(param, first, second, grad):
@@ -59,9 +65,7 @@
     weight_share = lax.psum_scatter(placed, "dp", scatter_dimension=0, tiled=True).astype(
         jnp.bfloat16
     )
-    weights = lax.all_gather(weight_share, "dp", axis=0, tiled=True).reshape(
-        row_count, feature_count
-    )
+    weights = push_the_cube(weight_share).reshape(row_count, feature_count)
     return (new_master[None], new_first[None], new_second[None], weights[None], grad_rms)
 
 

time: 831 us -> 767 us (0.923)
  waiting for transfers between devices: 682 us -> 592 us
  starting transfers between devices: 0.16 us -> 24.1 us
    all_gather x1 -> x0, waiting for transfers between devices: 141 us -> none  [shards(): lax.all_gather(weight_share, 'dp', axis=0, tiled=True)]
    all_to_all x0 -> x1, waiting for transfers between devices: none -> 50.8 us  [push_the_cube(): lax.all_to_all(jnp.stack([frame_in] * lax.axis_size('dp')), 'dp', 0, 0)]
    all_to_all x0 -> x1, starting transfers between devices: none -> 24 us  [push_the_cube(): lax.all_to_all(jnp.stack([frame_in] * lax.axis_size('dp')), 'dp', 0, 0)]
where the time goes in v1:
time: 767 us; the launch traced here: 764 us
  waiting for transfers between devices  592 us (77%)
  blocking collectives  113 us (15%)
  starting transfers between devices  24.1 us (3%)
  between operations  15.8 us (2%)
  local copies, waits for them, and re-layouts  13.3 us (2%)
    reduce_scatter x1, waiting for transfers between devices, shards(): lax.psum_scatter(flat_grad, 'dp', scatter_dimension=0, tiled=True)  258 us
    reduce_scatter x1, waiting for transfers between devices, shards(): lax.psum_scatter(placed, 'dp', scatter_dimension=0, tiled=True)  246 us
    psum x1, blocking collectives, shards(): squares = lax.psum(jnp.sum(grad_share * grad_share), ('dp', 'layer'))  113 us
    all_to_all x1, waiting for transfers between devices, push_the_cube(): lax.all_to_all(jnp.stack([frame_in] * lax.axis_size('dp')), 'dp', 0, 0)  50.8 us
    all_gather x1, waiting for transfers between devices, shards(): lax.all_gather(grad_share, 'dp', axis=0, tiled=True)  36.3 us
    all_to_all x1, starting transfers between devices, push_the_cube(): lax.all_to_all(jnp.stack([frame_in] * lax.axis_size('dp')), 'dp', 0, 0)  24 us
  transfers between devices with their start and end apart: 4, of which 4 were waited for; matrix products, arithmetic and copies ran while one was open for 0% of the time, Pallas kernels for 0%

profile of v1, /device:TPU:1, one launch (start us, length us, event | category | flops | bytes accessed | tf_op | source)
XLA Modules:
  0.0 763.8 jit_solution(6322918874845406969)
XLA Ops:
  7.2 0.0 reduce-scatter.3.cloned.1.call-start
  7.2 2.6 reshape.113
  9.8 0.0 reduce-scatter.3.cloned.1.call-update
  9.9 0.0 all-gather.2.cloned.1.call-start
  9.9 258.4 %reduce-scatter.3.cloned.1.call-done = f32[32,128]{1,0:T(8,128)} async-done(((f32[4096,128]{1,0:T(8,128)}), f32[32,128]{1,0:T(8,128)}) %reduce-scatter.3.cloned.1.call-update) | async-done | bytes 16400 | tf_op jit(solution)/shard_map/reduce_scatter | solution.py:40
  268.3 0.0 reduce-scatter.5.cloned.1.call-start
  268.4 0.1 select_reduce_fusion
  268.6 1.3 multiply_reduce_fusion
  269.9 113.3 %psum.7 = f32[]{:T(128)} all-reduce(f32[]{:T(128)} %multiply_reduce_fusion), channel_id=1, replica_groups=mesh['dp'=128,'layer'=4] {'dp','layer'}, use_global_device_ids=true, to_apply=%region_4.5 | all-reduce | flops 1 | bytes 8 | tf_op jit(solution)/shard_map/psum | solution.py:42
  384.0 36.3 %all-gather.2.cloned.1.call-done = f32[4096,128]{1,0:T(8,128)} async-done(((f32[32,128]{1,0:T(8,128)}), f32[4096,128]{1,0:T(8,128)}) %all-gather.2.cloned.1.call-update) | async-done | bytes 2097168 | tf_op jit(solution)/shard_map/all_gather | solution.py:41
  420.3 2.3 reshape_reshape.3
  422.6 0.6 gather_fusion
  423.2 0.3 fusion.9
  423.5 2.7 gather_fusion.1
  426.2 2.0 convert_select_fusion
  428.2 2.7 select_n.93
  430.9 246.3 %reduce-scatter.5.cloned.1.call-done = f32[32,128]{1,0:T(8,128)} async-done(((f32[4096,128]{1,0:T(8,128)}), f32[32,128]{1,0:T(8,128)}) %reduce-scatter.5.cloned.1.call-update) | async-done | bytes 16400 | tf_op jit(solution)/shard_map/reduce_scatter | solution.py:65
  677.2 0.7 convert_element_type.22
  677.9 1.1 stack.2
  679.0 24.0 %all-to-all-start = ((bf16[128,32,128]{2,1,0:T(8,128)(2,1)}), bf16[128,32,128]{2,1,0:T(8,128)(2,1)S(1)}, u32[]{:S(2)}, u32[]{:S(2)}) async-start(bf16[128,32,128]{2,1,0:T(8,128)(2,1)} %stack.2), calls=%async_computation.2 | async-start | bytes 2097152 | tf_op jit(solution)/shard_map/all_to_all | solution.py:16
  703.1 0.1 fusion.11
  703.2 1.0 broadcast_select_fusion.1
  704.1 50.8 %all-to-all-done = bf16[128,32,128]{2,1,0:T(8,128)(2,1)S(1)} async-done(((bf16[128,32,128]{2,1,0:T(8,128)(2,1)}), bf16[128,32,128]{2,1,0:T(8,128)(2,1)S(1)}, u32[]{:S(2)}, u32[]{:S(2)}) %all-to-all-start) | async-done | bytes 1048608 | tf_op jit(solution)/shard_map/all_to_all | solution.py:16
  754.9 1.3 broadcast_in_dim_reshape_reshape.3
  (19 shorter events, 0.1 us)
Async XLA Ops:
  7.2 261.2 %copy-start.4 = (s32[1,128]{1,0:T(1,128)S(1)}, s32[1,128]{1,0:T(1,128)}, u32[]{:S(2)}) copy-start(s32[1,128]{1,0:T(1,128)} %param.11) | copy-start | bytes 1540
  7.2 261.2 %copy-start.3 = (s32[1,128]{1,0:T(1,128)S(1)}, s32[1,128]{1,0:T(1,128)}, u32[]{:S(2)}) copy-start(s32[1,128]{1,0:T(1,128)} %param.10) | copy-start | bytes 1540
  7.2 261.1 %reduce-scatter.3.cloned.1.call-start = ((), (), s32[]{:S(2)}) async-start(), calls=%async_computation.3 | async-start | bytes 2113536 | tf_op jit(solution)/shard_map/reduce_scatter | solution.py:40
  9.9 410.4 %all-gather.2.cloned.1.call-start = ((), (), s32[]{:S(2)}) async-start(), calls=%async_computation.4 | async-start | bytes 2113536 | tf_op jit(solution)/shard_map/all_gather | solution.py:41
  268.3 408.9 %reduce-scatter.5.cloned.1.call-start = ((), (), s32[]{:S(2)}) async-start(), calls=%async_computation.5 | async-start | bytes 2113536 | tf_op jit(solution)/shard_map/reduce_scatter | solution.py:65
  383.9 39.3 %copy-start = (f32[1,3,2,2048]{3,2,1,0:T(2,128)S(1)}, f32[1,3,2,2048]{3,2,1,0:T(2,128)}, u32[]{:S(2)}) copy-start(f32[1,3,2,2048]{3,2,1,0:T(2,128)} %param.9) | copy-start | bytes 147460
  383.9 39.3 %copy-start.1 = (f32[1,3,2,2048]{3,2,1,0:T(2,128)S(1)}, f32[1,3,2,2048]{3,2,1,0:T(2,128)}, u32[]{:S(2)}) copy-start(f32[1,3,2,2048]{3,2,1,0:T(2,128)} %param.7) | copy-start | bytes 147460
  384.0 39.3 %copy-start.2 = (f32[1,3,2,2048]{3,2,1,0:T(2,128)S(1)}, f32[1,3,2,2048]{3,2,1,0:T(2,128)}, u32[]{:S(2)}) copy-start(f32[1,3,2,2048]{3,2,1,0:T(2,128)} %param.8) | copy-start | bytes 147460
  679.0 75.9 %all-to-all-start = ((bf16[128,32,128]{2,1,0:T(8,128)(2,1)}), bf16[128,32,128]{2,1,0:T(8,128)(2,1)S(1)}, u32[]{:S(2)}, u32[]{:S(2)}) async-start(bf16[128,32,128]{2,1,0:T(8,128)(2,1)} %stack.2), calls=%async_computation.2 | async-start | bytes 2097152 | tf_op jit(solution)/shard_map/all_to_all | solution.py:16
Sparse Core Ops, SparseCore 0:
  12.6 255.6 reduce-scatter.2
  271.4 148.7 all-gather.1
  431.1 246.0 reduce-scatter.4
